TPU v7x, 32 devices: a whole 2x2x4 slice. The times are simulated.
32 devices in a mesh: wide: 16 (over z, y, core), narrow: 2 (over x).
Axes of the slice: x: 2, y: 2, z: 4, core: 2. Of those that a mesh axis runs over, the one named last changes fastest.
Arguments:
- inputs: bfloat16 [2, 32, 128, 1024], P(None, ('wide', 'narrow')), may hold values from -6 to 6
- out_grad: bfloat16 [2, 32, 128, 1024], P(None, ('wide', 'narrow')), may hold values from -6 to 6
- group_id: int32 [2, 32], P(None, ('wide', 'narrow')), may hold values from 0 to 15
- group_count: int32 [16], replicated, may hold values from 1 to 4
- norm_gain: bfloat16 [4, 1024], P(None, 'narrow'), may hold values from 0.5 to 1.5
- norm_bias: bfloat16 [4, 1024], P(None, 'narrow'), may hold values from -1.25 to 1.25
- w_qkv: bfloat16 [1024, 3072], P('narrow'), may hold values from -0.1875 to 0.1875
- w_out: bfloat16 [1024, 1024], P('narrow'), may hold values from -1.5 to 1.5
- w_up: bfloat16 [1024, 4096], P('narrow'), may hold values from -0.1875 to 0.1875
- w_down: bfloat16 [4096, 1024], P('narrow'), may hold values from -0.09375 to 0.09375
- bias_model: bfloat16 [4, 1024], P(None, 'narrow'), may hold values from -0.625 to 0.625
- bias_up: bfloat16 [4096], P('narrow'), may hold values from -0.625 to 0.625
Outputs:
- output: bfloat16 [2, 32, 128, 1024], P(None, ('wide', 'narrow'))
- grad_input: bfloat16 [2, 32, 128, 1024], P(None, ('wide', 'narrow'))
- grad_norm_gain: float32 [4, 1024], P(None, 'narrow')
- grad_norm_bias: float32 [4, 1024], P(None, 'narrow')
- grad_qkv: float32 [1024, 3072], P('narrow')
- grad_out: float32 [1024, 1024], P('narrow')
- grad_up: float32 [1024, 4096], P('narrow')
- grad_down: float32 [4096, 1024], P('narrow')
- grad_bias_model: float32 [4, 1024], P(None, 'narrow')
- grad_bias_up: float32 [4096], P('narrow')
All inputs are finite; a program needn't handle non-finite values.
Results may differ from a plain program's by a relative error of at most 0.02.
Values may be sent and summed in bfloat16 or wider, within the bound.
No kernel may reach another device: no remote copies, remote signals or barrier semaphores. Data moves between devices by JAX's collectives and lax.ppermute only.
A program may use at most 256 MiB of HBM per device.

v0:
```python
import math
import jax
import jax.numpy as jnp
from jax import lax
from jax.sharding import PartitionSpec as P

HEADS = 16
EPSILON = 1e-05
RELAX = 32.0


def layer_norm(value, gain, shift):
    average = jnp.mean(value, axis=-1, keepdims=True)
    centred = value - average
    spread = jnp.mean(centred * centred, axis=-1, keepdims=True)
    return centred * lax.rsqrt(spread + EPSILON) * gain + shift


def exact_gelu(value):
    return jax.nn.gelu(value, approximate=False)


def forward_product(left, right):
    return jnp.dot(left, right, preferred_element_type=jnp.float32)


def back_product(grad, weight):
    return lax.dot_general(
        grad, weight, (((1,), (1,)), ((), ())), preferred_element_type=jnp.float32
    )


def weight_grad(left, grad):
    return lax.dot_general(left, grad, (((0,), (0,)), ((), ())), preferred_element_type=jnp.float32)


def column_sum(grad):
    return jnp.sum(grad.astype(jnp.float32), axis=0)


def split_heads(qkv, seqs, heads):
    length = qkv.shape[0] // seqs
    width = qkv.shape[1] // 3
    parts = qkv.reshape(seqs, length, 3, heads, width // heads)
    return (parts[:, :, 0], parts[:, :, 1], parts[:, :, 2])


def raw_scores(query, keys):
    length = query.shape[1]
    scale = RELAX * math.sqrt(query.shape[-1])
    scores = jnp.einsum("sqhd,skhd->shqk", query, keys, preferred_element_type=jnp.float32) / scale
    rows = lax.broadcasted_iota(jnp.int32, (length, length), 0)
    columns = lax.broadcasted_iota(jnp.int32, (length, length), 1)
    return jnp.where(columns <= rows, scores, -1000000000.0)


def forward_pass(block, full, seqs, heads):
    gain = full[0].astype(jnp.float32)
    shift = full[1].astype(jnp.float32)
    bias = full[6].astype(jnp.float32)
    bias_hidden = full[7].astype(jnp.float32)
    tokens, width = block.shape
    qkv_bias = jnp.concatenate([bias[0], jnp.zeros((width,), jnp.float32), bias[1]])
    block_value = block.astype(jnp.float32)
    first = layer_norm(block_value, gain[0], shift[0]).astype(jnp.bfloat16)
    qkv = (forward_product(first, full[2]) + qkv_bias).astype(jnp.bfloat16)
    query, keys, values = split_heads(qkv, seqs, heads)
    scores = raw_scores(query, keys)
    top = jnp.max(scores, axis=-1, keepdims=True)
    exps = jnp.exp(RELAX * (scores - top))
    total = jnp.sum(exps, axis=-1, keepdims=True)
    logsum = jnp.log(total)
    weights = (exps / total).astype(jnp.bfloat16)
    mixed = jnp.einsum("shqk,skhd->sqhd", weights, values, preferred_element_type=jnp.float32)
    mixed = mixed.reshape(tokens, width).astype(jnp.bfloat16)
    branch = forward_product(mixed, full[3]) + bias[2]
    middle = block_value + layer_norm(branch, gain[1], shift[1])
    third = layer_norm(middle, gain[2], shift[2]).astype(jnp.bfloat16)
    hidden = forward_product(third, full[4]) + bias_hidden
    active = exact_gelu(hidden).astype(jnp.bfloat16)
    second = forward_product(active, full[5]) + bias[3]
    result = middle + layer_norm(second, gain[3], shift[3])
    kept = (
        block_value,
        first,
        qkv,
        top,
        logsum,
        mixed,
        branch,
        middle,
        third,
        hidden,
        active,
        second,
    )
    return (result, kept)


def attention_back(qkv, top, logsum, grad_mixed, seqs, heads):
    query, keys, values = split_heads(qkv, seqs, heads)
    scores = raw_scores(query, keys)
    probs = jnp.exp(RELAX * (scores - top) - logsum)
    weights = probs.astype(jnp.bfloat16)
    tokens, width = grad_mixed.shape
    grad_heads = grad_mixed.reshape(seqs, tokens // seqs, heads, width // heads)
    grad_weights = jnp.einsum(
        "sqhd,skhd->shqk", grad_heads, values, preferred_element_type=jnp.float32
    )
    inner = jnp.sum(probs * grad_weights, axis=-1, keepdims=True)
    grad_scores = (RELAX * probs * (grad_weights - inner)).astype(jnp.bfloat16)
    scale = RELAX * math.sqrt(query.shape[-1])
    grad_query = (
        jnp.einsum("shqk,skhd->sqhd", grad_scores, keys, preferred_element_type=jnp.float32) / scale
    )
    grad_keys = (
        jnp.einsum("shqk,sqhd->skhd", grad_scores, query, preferred_element_type=jnp.float32)
        / scale
    )
    grad_values = jnp.einsum(
        "shqk,sqhd->skhd", weights, grad_heads, preferred_element_type=jnp.float32
    )
    stacked = jnp.stack([grad_query, grad_keys, grad_values], axis=2)
    return stacked.reshape(tokens, 3 * width).astype(jnp.bfloat16)


def backward_pass(cotangent, full, kept, seqs, heads):
    block_value, first, qkv, top, logsum, mixed, branch, middle, third, hidden, active, second = (
        kept
    )
    gain = full[0].astype(jnp.float32)
    shift = full[1].astype(jnp.float32)
    width = block_value.shape[1]
    unused_last, pull_last = jax.vjp(layer_norm, second, gain[3], shift[3])
    grad_second, gain_last, shift_last = pull_last(cotangent)
    grad_second = grad_second.astype(jnp.bfloat16)
    grad_down = weight_grad(active, grad_second)
    bias_down = column_sum(grad_second)
    grad_active = back_product(grad_second, full[5])
    unused_gelu, pull_gelu = jax.vjp(exact_gelu, hidden)
    grad_hidden = pull_gelu(grad_active)[0].astype(jnp.bfloat16)
    grad_up = weight_grad(third, grad_hidden)
    bias_hidden = column_sum(grad_hidden)
    grad_third = back_product(grad_hidden, full[4])
    unused_third, pull_third = jax.vjp(layer_norm, middle, gain[2], shift[2])
    grad_inner, gain_third, shift_third = pull_third(grad_third)
    grad_middle = cotangent + grad_inner
    unused_branch, pull_branch = jax.vjp(layer_norm, branch, gain[1], shift[1])
    grad_branch, gain_branch, shift_branch = pull_branch(grad_middle)
    grad_branch = grad_branch.astype(jnp.bfloat16)
    grad_out = weight_grad(mixed, grad_branch)
    bias_out = column_sum(grad_branch)
    grad_mixed = back_product(grad_branch, full[3]).astype(jnp.bfloat16)
    grad_qkv = attention_back(qkv, top, logsum, grad_mixed, seqs, heads)
    grad_project = weight_grad(first, grad_qkv)
    qkv_sums = column_sum(grad_qkv)
    grad_first = back_product(grad_qkv, full[2])
    unused_first, pull_first = jax.vjp(layer_norm, block_value, gain[0], shift[0])
    grad_block, gain_first, shift_first = pull_first(grad_first)
    grad_input = grad_middle + grad_block
    grad_gain = jnp.stack([gain_first, gain_branch, gain_third, gain_last])
    grad_shift = jnp.stack([shift_first, shift_branch, shift_third, shift_last])
    grad_bias = jnp.stack([qkv_sums[:width], qkv_sums[2 * width :], bias_out, bias_down])
    return (
        grad_input,
        (grad_gain, grad_shift, grad_project, grad_out, grad_up, grad_down, grad_bias, bias_hidden),
    )


def on_device(
    inputs,
    out_grad,
    group_id,
    group_count,
    norm_gain,
    norm_bias,
    w_qkv,
    w_out,
    w_up,
    w_down,
    bias_model,
    bias_up,
):
    micros, seqs, length, width = inputs.shape
    heads = HEADS
    tokens = seqs * length
    matches = (
        group_id[:, :, None] == jnp.arange(group_count.shape[0], dtype=jnp.int32)[None, None, :]
    )
    counts = jnp.sum(jnp.where(matches, group_count[None, None, :], 0), axis=-1)
    seq_scale = 1.0 / counts.astype(jnp.float32)
    results = []
    grad_inputs = []
    totals = None
    for micro in range(micros):
        full = (
            lax.all_gather(norm_gain, "narrow", axis=1, tiled=True),
            lax.all_gather(norm_bias, "narrow", axis=1, tiled=True),
            lax.all_gather(w_qkv, "narrow", axis=0, tiled=True),
            lax.all_gather(w_out, "narrow", axis=0, tiled=True),
            lax.all_gather(w_up, "narrow", axis=0, tiled=True),
            lax.all_gather(w_down, "narrow", axis=0, tiled=True),
            lax.all_gather(bias_model, "narrow", axis=1, tiled=True),
            lax.all_gather(bias_up, "narrow", axis=0, tiled=True),
        )
        result, kept = forward_pass(inputs[micro].reshape(tokens, width), full, seqs, heads)
        results.append(result.reshape(seqs, length, width).astype(jnp.bfloat16))
        full = (
            lax.all_gather(norm_gain, "narrow", axis=1, tiled=True),
            lax.all_gather(norm_bias, "narrow", axis=1, tiled=True),
            lax.all_gather(w_qkv, "narrow", axis=0, tiled=True),
            lax.all_gather(w_out, "narrow", axis=0, tiled=True),
            lax.all_gather(w_up, "narrow", axis=0, tiled=True),
            lax.all_gather(w_down, "narrow", axis=0, tiled=True),
            lax.all_gather(bias_model, "narrow", axis=1, tiled=True),
            lax.all_gather(bias_up, "narrow", axis=0, tiled=True),
        )
        cotangent = out_grad[micro].astype(jnp.float32) * seq_scale[micro][:, None, None]
        grad_input, grads = backward_pass(cotangent.reshape(tokens, width), full, kept, seqs, heads)
        grad_inputs.append(grad_input.reshape(seqs, length, width).astype(jnp.bfloat16))
        shares = (
            lax.psum_scatter(
                grads[0].astype(jnp.bfloat16), "narrow", scatter_dimension=1, tiled=True
            ).astype(jnp.float32),
            lax.psum_scatter(
                grads[1].astype(jnp.bfloat16), "narrow", scatter_dimension=1, tiled=True
            ).astype(jnp.float32),
            lax.psum_scatter(
                grads[2].astype(jnp.bfloat16), "narrow", scatter_dimension=0, tiled=True
            ).astype(jnp.float32),
            lax.psum_scatter(
                grads[3].astype(jnp.bfloat16), "narrow", scatter_dimension=0, tiled=True
            ).astype(jnp.float32),
            lax.psum_scatter(
                grads[4].astype(jnp.bfloat16), "narrow", scatter_dimension=0, tiled=True
            ).astype(jnp.float32),
            lax.psum_scatter(
                grads[5].astype(jnp.bfloat16), "narrow", scatter_dimension=0, tiled=True
            ).astype(jnp.float32),
            lax.psum_scatter(
                grads[6].astype(jnp.bfloat16), "narrow", scatter_dimension=1, tiled=True
            ).astype(jnp.float32),
            lax.psum_scatter(
                grads[7].astype(jnp.bfloat16), "narrow", scatter_dimension=0, tiled=True
            ).astype(jnp.float32),
        )
        if totals is None:
            totals = tuple(shares)
        else:
            totals = tuple((left + right for left, right in zip(totals, shares)))
    summed = (
        lax.psum(totals[0].astype(jnp.bfloat16), "wide").astype(jnp.float32),
        lax.psum(totals[1].astype(jnp.bfloat16), "wide").astype(jnp.float32),
        lax.psum(totals[2].astype(jnp.bfloat16), "wide").astype(jnp.float32),
        lax.psum(totals[3].astype(jnp.bfloat16), "wide").astype(jnp.float32),
        lax.psum(totals[4].astype(jnp.bfloat16), "wide").astype(jnp.float32),
        lax.psum(totals[5].astype(jnp.bfloat16), "wide").astype(jnp.float32),
        lax.psum(totals[6].astype(jnp.bfloat16), "wide").astype(jnp.float32),
        lax.psum(totals[7].astype(jnp.bfloat16), "wide").astype(jnp.float32),
    )
    output = jnp.stack(results)
    grad_all = jnp.stack(grad_inputs)
    return (
        output,
        grad_all,
        summed[0],
        summed[1],
        summed[2],
        summed[3],
        summed[4],
        summed[5],
        summed[6],
        summed[7],
    )


def solution(mesh):
    return jax.shard_map(
        on_device,
        mesh=mesh,
        in_specs=(
            P(None, ("wide", "narrow"), None, None),
            P(None, ("wide", "narrow"), None, None),
            P(None, ("wide", "narrow")),
            P(),
            P(None, "narrow"),
            P(None, "narrow"),
            P("narrow", None),
            P("narrow", None),
            P("narrow", None),
            P("narrow", None),
            P(None, "narrow"),
            P("narrow"),
        ),
        out_specs=(
            P(None, ("wide", "narrow"), None, None),
            P(None, ("wide", "narrow"), None, None),
            P(None, "narrow"),
            P(None, "narrow"),
            P("narrow", None),
            P("narrow", None),
            P("narrow", None),
            P("narrow", None),
            P(None, "narrow"),
            P("narrow"),
        ),
        check_vma=False,
    )
```

profile of v0, /device:TPU:0, one launch (start us, length us, event | category | flops | bytes accessed | tf_op | source)
XLA Modules:
  0.0 1364.5 jit_solution(11387868374793793821)
XLA Ops:
  10.1 5.3 all_gather.19
  30.1 62.6 %all-gather.5.cloned.1.call-done = bf16[1024,3072]{1,0:T(8,128)(2,1)} async-done(((bf16[512,3072]{1,0:T(8,128)(2,1)}), bf16[1024,3072]{1,0:T(8,128)(2,1)}) %all-gather.5.cloned.1.call-update) | async-done | bytes 6291472 | tf_op jit(solution)/shard_map/all_gather | solution.py:199
  104.4 23.1 %all-gather.7.cloned.1.call-done = bf16[1024,1024]{1,0:T(8,128)(2,1)} async-done(((bf16[512,1024]{1,0:T(8,128)(2,1)}), bf16[1024,1024]{1,0:T(8,128)(2,1)}) %all-gather.7.cloned.1.call-update) | async-done | bytes 2097168 | tf_op jit(solution)/shard_map/all_gather | solution.py:200
  138.8 94.2 %all-gather.9.cloned.1.call-done = bf16[1024,4096]{1,0:T(8,128)(2,1)} async-done(((bf16[512,4096]{1,0:T(8,128)(2,1)}), bf16[1024,4096]{1,0:T(8,128)(2,1)}) %all-gather.9.cloned.1.call-update) | async-done | bytes 8388624 | tf_op jit(solution)/shard_map/all_gather | solution.py:201
  233.0 9.9 multiply_convert_fusion
  242.9 95.5 %all-gather.11.cloned.1.call-done = bf16[4096,1024]{1,0:T(8,128)(2,1)} async-done(((bf16[2048,1024]{1,0:T(8,128)(2,1)}), bf16[4096,1024]{1,0:T(8,128)(2,1)}) %all-gather.11.cloned.1.call-update) | async-done | bytes 8388624 | tf_op jit(solution)/shard_map/all_gather | solution.py:202
  338.4 5.2 fusion.153
  344.5 9.1 multiply_convert_fusion.1
  360.7 5.7 fusion.126
  369.4 5.7 fusion.125
  420.1 7.1 convolution_convert_fusion.2
  427.2 7.2 convolution_convert_fusion.3
  435.7 5.6 convolution_convert_fusion
  442.6 5.6 convolution_convert_fusion.1
  470.9 62.1 %reduce-scatter.29.cloned.1.call-done = bf16[512,3072]{1,0:T(8,128)(2,1)} async-done(((bf16[1024,3072]{1,0:T(8,128)(2,1)}), bf16[512,3072]{1,0:T(8,128)(2,1)}) %reduce-scatter.29.cloned.1.call-update) | async-done | bytes 3145744 | tf_op jit(solution)/shard_map/reduce_scatter | solution.py:228
  533.0 79.5 %reduce-scatter.27.cloned.1.call-done = bf16[512,3072]{1,0:T(8,128)(2,1)} async-done(((bf16[1024,3072]{1,0:T(8,128)(2,1)}), bf16[512,3072]{1,0:T(8,128)(2,1)}) %reduce-scatter.27.cloned.1.call-update) | async-done | bytes 3145744 | tf_op jit(solution)/shard_map/reduce_scatter | solution.py:228
  612.5 5.7 add_convert_fusion.2
  618.2 96.6 %reduce-scatter.37.cloned.1.call-done = bf16[512,4096]{1,0:T(8,128)(2,1)} async-done(((bf16[1024,4096]{1,0:T(8,128)(2,1)}), bf16[512,4096]{1,0:T(8,128)(2,1)}) %reduce-scatter.37.cloned.1.call-update) | async-done | bytes 4194320 | tf_op jit(solution)/shard_map/reduce_scatter | solution.py:234
  714.7 102.1 %reduce-scatter.35.cloned.1.call-done = bf16[512,4096]{1,0:T(8,128)(2,1)} async-done(((bf16[1024,4096]{1,0:T(8,128)(2,1)}), bf16[512,4096]{1,0:T(8,128)(2,1)}) %reduce-scatter.35.cloned.1.call-update) | async-done | bytes 4194320 | tf_op jit(solution)/shard_map/reduce_scatter | solution.py:234
  816.8 7.2 add_convert_fusion.1
  824.1 94.4 %reduce-scatter.41.cloned.1.call-done = bf16[2048,1024]{1,0:T(8,128)(2,1)} async-done(((bf16[4096,1024]{1,0:T(8,128)(2,1)}), bf16[2048,1024]{1,0:T(8,128)(2,1)}) %reduce-scatter.41.cloned.1.call-update) | async-done | bytes 4194320 | tf_op jit(solution)/shard_map/reduce_scatter | solution.py:237
  918.5 101.5 %reduce-scatter.39.cloned.1.call-done = bf16[2048,1024]{1,0:T(8,128)(2,1)} async-done(((bf16[4096,1024]{1,0:T(8,128)(2,1)}), bf16[2048,1024]{1,0:T(8,128)(2,1)}) %reduce-scatter.39.cloned.1.call-update) | async-done | bytes 4194320 | tf_op jit(solution)/shard_map/reduce_scatter | solution.py:237
  1020.0 7.6 add_convert_fusion
  1029.5 6.9 all-reduce.4
  1039.5 8.4 reduce-scatter.43.cloned.1.call-done
  1048.9 12.9 reduce-scatter.49.cloned.1.call-done
  1062.8 12.9 reduce-scatter.47.cloned.1.call-done
  1076.7 12.9 reduce-scatter.53.cloned.1.call-done
  1090.5 12.9 reduce-scatter.51.cloned.1.call-done
  1104.5 64.5 %all-reduce.2 = (bf16[4,512]{1,0:T(4,128)(2,1)S(1)}, bf16[4,512]{1,0:T(4,128)(2,1)S(1)}, bf16[4,512]{1,0:T(4,128)(2,1)S(1)}, bf16[2048]{0:T(1024)(128)(2,1)S(1)}) all-reduce(bf16[4,512]{1,0:T(4,128)(2,1)S(1)} %add_convert_fusion.19, bf16[4,512]{1,0:T(4,128)(2,1)S(1)} %add_convert_fusion.18, ...), channel_id=1, replica_groups=mesh['wide'=16,'narrow'=2] {'wide'}, use_global_device_ids=true, to_apply=%region_49.50 | all-reduce | flops 8192 | bytes 32768 | tf_op jit(solution)/shard_map/psum | solution.py:252
  1171.4 170.0 %all-reduce.7.cloned.1.call-done = (bf16[512,3072]{1,0:T(8,128)(2,1)}, bf16[512,1024]{1,0:T(8,128)(2,1)}, bf16[512,4096]{1,0:T(8,128)(2,1)}, bf16[2048,1024]{1,0:T(8,128)(2,1)}) async-done(((bf16[512,3072]{1,0:T(8,128)(2,1)}, bf16[512,1024]{1,0:T(8,128)(2,1)}, bf16[512,4096]{1,0:T(8,128)(2,1)}, bf16[2048,1024]{1,0:T(8,128)(2,1)}), (bf16[512,3072]{1,0:T(8,128)(2,1)}, bf16[512,1024]{1,0:T(8,128)(2,1)}, ...) | async-done | bytes 12582928 | tf_op jit(solution)/shard_map/psum | solution.py:254
  1341.4 5.5 convert_element_type.454
  (335 shorter events, 142.7 us)
Async XLA Ops:
  7.2 85.5 %all-gather.5.cloned.1.call-start = ((), (), s32[]{:S(2)}) async-start(), calls=%async_computation.14 | async-start | bytes 9437184 | tf_op jit(solution)/shard_map/all_gather | solution.py:199
  7.9 119.5 %all-gather.7.cloned.1.call-start = ((), (), s32[]{:S(2)}) async-start(), calls=%async_computation.15 | async-start | bytes 3145728 | tf_op jit(solution)/shard_map/all_gather | solution.py:200
  8.7 224.3 %all-gather.9.cloned.1.call-start = ((), (), s32[]{:S(2)}) async-start(), calls=%async_computation.16 | async-start | bytes 12582912 | tf_op jit(solution)/shard_map/all_gather | solution.py:201
  9.4 10.4 copy-start.48
  9.4 14.7 %copy-start.49 = (bf16[4,512]{1,0:T(4,128)(2,1)S(1)}, bf16[4,512]{1,0:T(4,128)(2,1)}, u32[]{:S(2)}) copy-start(bf16[4,512]{1,0:T(4,128)(2,1)} %param.16) | copy-start | bytes 12292
  9.4 19.3 %copy-start.2 = (bf16[2,1,128,1024]{3,2,1,0:T(8,128)(2,1)S(1)}, bf16[2,1,128,1024]{3,2,1,0:T(8,128)(2,1)}, u32[]{:S(2)}) copy-start(bf16[2,1,128,1024]{3,2,1,0:T(8,128)(2,1)} %param.12) | copy-start | bytes 1572868
  9.4 19.4 %copy-start.60 = (s32[16]{0:T(128)S(1)}, s32[16]{0:T(128)}, u32[]{:S(2)}) copy-start(s32[16]{0:T(128)} %param.15) | copy-start | bytes 196
  9.5 19.4 %copy-start.61 = (s32[2,1]{0,1:T(1,128)S(1)}, s32[2,1]{0,1:T(1,128)}, u32[]{:S(2)}) copy-start(s32[2,1]{0,1:T(1,128)} %param.14) | copy-start | bytes 28
  9.5 328.9 %all-gather.11.cloned.1.call-start = ((), (), s32[]{:S(2)}) async-start(), calls=%async_computation.17 | async-start | bytes 12582912 | tf_op jit(solution)/shard_map/all_gather | solution.py:202
  10.0 457.9 %reduce-scatter.33.cloned.1.call-start = ((), (), s32[]{:S(2)}) async-start(), calls=%async_computation.21 | async-start | bytes 3145728 | tf_op jit(solution)/shard_map/reduce_scatter | solution.py:231
  29.4 67.2 %copy-start.52 = (f32[128]{0:T(128)}, f32[128]{0:T(128)S(1)}, u32[]{:S(2)}) copy-start(f32[128]{0:T(128)S(1)} %get-tuple-element.41) | copy-start | bytes 1540
  101.5 30.6 %copy-start.20 = (bf16[128,3072]{0,1:T(8,128)(2,1)}, bf16[128,3072]{0,1:T(8,128)(2,1)S(1)}, u32[]{:S(2)}) copy-start(bf16[128,3072]{0,1:T(8,128)(2,1)S(1)} %copy.66) | copy-start | bytes 2359300
  104.4 27.7 %copy-start.34 = (bf16[16,64,128]{2,1,0:T(8,128)(2,1)}, bf16[16,64,128]{2,1,0:T(8,128)(2,1)S(1)}, u32[]{:S(2)}) copy-start(bf16[16,64,128]{2,1,0:T(8,128)(2,1)S(1)} %convolution_convert_fusion.11) | copy-start | bytes 786436
  137.0 105.9 %copy-start.56 = (f32[128]{0:T(128)}, f32[128]{0:T(128)S(1)}, u32[]{:S(2)}) copy-start(f32[128]{0:T(128)S(1)} %multiply_reduce_fusion.14) | copy-start | bytes 1540
  138.8 104.2 %copy-start.58 = (f32[128]{0:T(128)}, f32[128]{0:T(128)S(1)}, u32[]{:S(2)}) copy-start(f32[128]{0:T(128)S(1)} %multiply_reduce_fusion.16) | copy-start | bytes 1540
  338.4 16.2 %slice-start = ((s8[8388608]{0:T(1024)(128)(4,1)}), s8[4194304]{0:T(1024)(128)(4,1)S(1)}, s32[]{:S(2)}) async-start(s8[8388608]{0:T(1024)(128)(4,1)} %bitcast.286), calls=%async_computation.33 | async-start | bytes 8388608
  344.5 10.1 slice-start.1
  386.9 81.1 %reduce-scatter.31.cloned.1.call-start = ((), (), s32[]{:S(2)}) async-start(), calls=%async_computation.20 | async-start | bytes 3145728 | tf_op jit(solution)/shard_map/reduce_scatter | solution.py:231
  391.1 141.9 %reduce-scatter.29.cloned.1.call-start = ((), (), s32[]{:S(2)}) async-start(), calls=%async_computation.19 | async-start | bytes 9437184 | tf_op jit(solution)/shard_map/reduce_scatter | solution.py:228
  407.5 205.0 %reduce-scatter.27.cloned.1.call-start = ((), (), s32[]{:S(2)}) async-start(), calls=%async_computation.18 | async-start | bytes 9437184 | tf_op jit(solution)/shard_map/reduce_scatter | solution.py:228
  419.1 295.7 %reduce-scatter.37.cloned.1.call-start = ((), (), s32[]{:S(2)}) async-start(), calls=%async_computation.23 | async-start | bytes 12582912 | tf_op jit(solution)/shard_map/reduce_scatter | solution.py:234
  427.2 389.6 %reduce-scatter.35.cloned.1.call-start = ((), (), s32[]{:S(2)}) async-start(), calls=%async_computation.22 | async-start | bytes 12582912 | tf_op jit(solution)/shard_map/reduce_scatter | solution.py:234
  434.5 484.0 %reduce-scatter.41.cloned.1.call-start = ((), (), s32[]{:S(2)}) async-start(), calls=%async_computation.25 | async-start | bytes 12582912 | tf_op jit(solution)/shard_map/reduce_scatter | solution.py:237
  441.3 578.7 %reduce-scatter.39.cloned.1.call-start = ((), (), s32[]{:S(2)}) async-start(), calls=%async_computation.24 | async-start | bytes 12582912 | tf_op jit(solution)/shard_map/reduce_scatter | solution.py:237
  448.2 590.3 %reduce-scatter.45.cloned.1.call-start = ((), (), s32[]{:S(2)}) async-start(), calls=%async_computation.27 | async-start | bytes 393216
  462.5 585.4 %reduce-scatter.43.cloned.1.call-start = ((), (), s32[]{:S(2)}) async-start(), calls=%async_computation.26 | async-start | bytes 393216
  463.5 598.3 %reduce-scatter.49.cloned.1.call-start = ((), (), s32[]{:S(2)}) async-start(), calls=%async_computation.29 | async-start | bytes 393216
  464.5 611.1 %reduce-scatter.47.cloned.1.call-start = ((), (), s32[]{:S(2)}) async-start(), calls=%async_computation.28 | async-start | bytes 393216
  465.7 623.8 %reduce-scatter.53.cloned.1.call-start = ((), (), s32[]{:S(2)}) async-start(), calls=%async_computation.31 | async-start | bytes 393216
  466.9 636.5 %reduce-scatter.51.cloned.1.call-start = ((), (), s32[]{:S(2)}) async-start(), calls=%async_computation.30 | async-start | bytes 393216
  467.9 873.5 %all-reduce.7.cloned.1.call-start = ((), (), s32[]{:S(2)}) async-start(), calls=%async_computation.32 | async-start | bytes 25165824 | tf_op jit(solution)/shard_map/psum | solution.py:254
  1027.6 9.7 copy-start.23
  (52 other events, 163.1 us)
Sparse Core Ops, SparseCore 0:
  9.5 83.1 all-gather.4
  94.2 33.1 all-gather.6
  129.0 103.9 all-gather.8
  234.4 103.9 all-gather.10
  387.0 31.8 reduce-scatter.32
  421.0 31.8 reduce-scatter.30
  455.8 77.1 reduce-scatter.28
  535.3 77.1 reduce-scatter.26
  615.4 99.3 reduce-scatter.36
  717.4 99.3 reduce-scatter.34
  819.1 99.3 reduce-scatter.40
  920.6 99.3 reduce-scatter.38
  1022.2 11.7 reduce-scatter.44
  1036.1 11.7 reduce-scatter.42
  1050.0 11.7 reduce-scatter.48
  1063.9 11.7 reduce-scatter.46
  1077.7 11.7 reduce-scatter.52
  1091.6 11.7 reduce-scatter.50
  1108.6 232.8 all-reduce.6
where the time goes:
time: 1370 us; the launch traced here: 1360 us
  waiting for transfers between devices  1040 us (76%)
  matrix products  125 us (9%)
  blocking collectives  90 us (7%)
  other arithmetic  59 us (4%)
  local copies, waits for them, and re-layouts  28.8 us (2%)
  between operations  16.4 us (1%)
    reduce_scatter x2, waiting for transfers between devices, on_device(): lax.psum_scatter(grads[4].astype(jnp.bfloat16), 'narrow', scatter_dimensi...  199 us
    reduce_scatter x2, waiting for transfers between devices, on_device(): lax.psum_scatter(grads[5].astype(jnp.bfloat16), 'narrow', scatter_dimensi...  196 us
    psum x1, waiting for transfers between devices, on_device(): lax.psum(totals[2].astype(jnp.bfloat16), 'wide').astype(jnp.float32)  170 us
    reduce_scatter x2, waiting for transfers between devices, on_device(): lax.psum_scatter(grads[2].astype(jnp.bfloat16), 'narrow', scatter_dimensi...  142 us
    all_gather x1, waiting for transfers between devices, on_device(): lax.all_gather(w_down, 'narrow', axis=0, tiled=True)  95.5 us
    all_gather x1, waiting for transfers between devices, on_device(): lax.all_gather(w_up, 'narrow', axis=0, tiled=True)  94.2 us
    psum x1, blocking collectives, on_device(): lax.psum(totals[0].astype(jnp.bfloat16), 'wide').astype(jnp.float32)  64.5 us
    unnamed x25, waiting for transfers between devices  62.7 us
  transfers between devices with their start and end apart: 19, of which 16 were waited for; matrix products, arithmetic and copies ran while one was open for 10% of the time, Pallas kernels for 0%

commit v1 on v0

--- a/solution.py
+++ b/solution.py
@@ -7,6 +7,28 @@
 HEADS = 16
 EPSILON = 1e-05
 RELAX = 32.0
+
+
+def in_order(tiles, dim):
+    tiles = jnp.moveaxis(tiles, 0, dim)
+    shape = tiles.shape
+    return tiles.reshape(*shape[:dim], shape[dim] * shape[dim + 1], *shape[dim + 2 :])
+
+
+def doubled(array, axis):
+    length = lax.axis_size(axis)
+    parts = array[None]
+    for level in range(length.bit_length() - 1):
+        bit = 1 << level
+        other = lax.ppermute(parts, axis, [(i, i ^ bit) for i in range(length)])
+        both = jnp.stack([parts, other])
+        upper = lax.axis_index(axis) >> level & 1
+        parts = jnp.where(upper == 0, both, both[::-1]).reshape(-1, *array.shape)
+    return parts
+
+
+def gather_by_bits(x, axis, dim):
+    return in_order(doubled(x, axis), dim)
 
 
 def layer_norm(value, gain, shift):
@@ -198,7 +220,7 @@
             lax.all_gather(norm_bias, "narrow", axis=1, tiled=True),
             lax.all_gather(w_qkv, "narrow", axis=0, tiled=True),
             lax.all_gather(w_out, "narrow", axis=0, tiled=True),
-            lax.all_gather(w_up, "narrow", axis=0, tiled=True),
+            gather_by_bits(w_up, "narrow", 0),
             lax.all_gather(w_down, "narrow", axis=0, tiled=True),
             lax.all_gather(bias_model, "narrow", axis=1, tiled=True),
             lax.all_gather(bias_up, "narrow", axis=0, tiled=True),

time: 1370 us -> 1420 us (1.036)
  blocking collectives: 90 us -> 243 us
  waiting for transfers between devices: 1040 us -> 889 us
  other arithmetic: 59 us -> 83 us
  matrix products: 125 us -> 143 us
    all_gather x1, blocking collectives: 4.36 us -> 158 us  [on_device(): lax.all_gather(bias_up, 'narrow', axis=0, tiled=True)]
    all_gather x1, waiting for transfers between devices: 62.6 us -> 0.01 us  [on_device(): lax.all_gather(w_qkv, 'narrow', axis=0, tiled=True)]
    all_gather x1, waiting for transfers between devices: 95.5 us -> 35.2 us  [on_device(): lax.all_gather(w_down, 'narrow', axis=0, tiled=True)]
    all_gather x1, waiting for transfers between devices: 23.1 us -> 0.02 us  [on_device(): lax.all_gather(w_out, 'narrow', axis=0, tiled=True)]
    dot_general x8, matrix products: 36.4 us -> 51.4 us  [forward_product(): return jnp.dot(left, right, preferred_element_type=jnp.float32)]
    select_n x0 -> x1, other arithmetic: none -> 14.6 us  [doubled(): parts = jnp.where(upper == 0, both, both[::-1]).reshape(-1, *array.shape)]
  transfers between devices with their start and end apart: 19 -> 20, of which waited for: 16 -> 14; matrix products, arithmetic and copies ran while one was open for 10% -> 15% of each run, Pallas kernels for 0% -> 0%
where the time goes in v1:
time: 1420 us; the launch traced here: 1410 us
  waiting for transfers between devices  889 us (63%)
  blocking collectives  243 us (17%)
  matrix products  143 us (10%)
  other arithmetic  83 us (6%)
  local copies, waits for them, and re-layouts  31 us (2%)
  between operations  16.3 us (1%)
    reduce_scatter x2, waiting for transfers between devices, on_device(): lax.psum_scatter(grads[4].astype(jnp.bfloat16), 'narrow', scatter_dimensi...  199 us
    reduce_scatter x2, waiting for transfers between devices, on_device(): lax.psum_scatter(grads[5].astype(jnp.bfloat16), 'narrow', scatter_dimensi...  196 us
    psum x1, waiting for transfers between devices, on_device(): lax.psum(totals[2].astype(jnp.bfloat16), 'wide').astype(jnp.float32)  170 us
    all_gather x1, blocking collectives, on_device(): lax.all_gather(bias_up, 'narrow', axis=0, tiled=True)  158 us
    reduce_scatter x2, waiting for transfers between devices, on_device(): lax.psum_scatter(grads[2].astype(jnp.bfloat16), 'narrow', scatter_dimensi...  141 us
    all_gather x1, waiting for transfers between devices, on_device(): lax.all_gather(w_up, 'narrow', axis=0, tiled=True)  86.3 us
    psum x1, blocking collectives, on_device(): lax.psum(totals[0].astype(jnp.bfloat16), 'wide').astype(jnp.float32)  64.1 us
    unnamed x25, waiting for transfers between devices  62.2 us
  transfers between devices with their start and end apart: 20, of which 14 were waited for; matrix products, arithmetic and copies ran while one was open for 15% of the time, Pallas kernels for 0%

profile of v1, /device:TPU:0, one launch (start us, length us, event | category | flops | bytes accessed | tf_op | source)
XLA Modules:
  0.0 1410.1 jit_solution(13239620144524256360)
XLA Ops:
  12.6 158.3 %all_gather.21 = bf16[4096]{0:T(1024)(128)(2,1)S(1)} all-gather(bf16[2048]{0:T(1024)(128)(2,1)S(1)} %copy-done.53), channel_id=1, replica_groups=mesh['wide'=16,'narrow'=2] {'narrow'}, dimensions={0}, use_global_device_ids=true | all-gather | bytes 12288 | tf_op jit(solution)/shard_map/all_gather | solution.py:226
  186.6 7.6 pad_maximum_fusion
  194.2 14.6 %reverse_select_fusion = bf16[2,1,512,4096]{3,2,1,0:T(8,128)(2,1)} fusion(bf16[2,1,512,4096]{3,2,1,0:T(8,128)(2,1)} %pad_maximum_fusion, pred[]{:T(512)S(6)} %eq.25), kind=kLoop, calls=%fused_computation.2 | loop fusion | flops 4194304 | bytes 16777216 | tf_op jit(solution)/shard_map/jit(_where)/select_n | solution.py:26
  234.2 22.5 %multiply_convert_fusion = (bf16[128,4096]{1,0:T(8,128)(2,1)}, f32[128,4096]{1,0:T(8,128)}, f32[128,4096]{1,0:T(8,128)}) fusion(f32[4096]{0:T(1024)S(1)} %convert_element_type.401, bf16[1024,4096]{1,0:T(8,128)(2,1)} %bitcast.294, f32[128,1024]{1,0:T(8,128)S(1)} %get-tuple-element.93, f32[128]{0:T(128)S(1)} %fusion.113, ...), kind=kOutput, calls=%fused_computation.26 | convolution fusion | flops 1109000192 | bytes 14181376 | tf_op jit(solution)/shard_map/dot_general | solution.py:46
  256.8 8.9 multiply_convert_fusion.1
  265.7 35.2 %all-gather.9.cloned.1.call-done = bf16[4096,1024]{1,0:T(8,128)(2,1)} async-done(((bf16[2048,1024]{1,0:T(8,128)(2,1)}), bf16[4096,1024]{1,0:T(8,128)(2,1)}) %all-gather.9.cloned.1.call-update) | async-done | bytes 8388624 | tf_op jit(solution)/shard_map/all_gather | solution.py:224
  300.9 5.2 fusion.153
  320.0 86.3 %all-gather.11.cloned.1.call-done = bf16[1024,4096]{1,0:T(8,128)(2,1)} async-done(((bf16[512,4096]{1,0:T(8,128)(2,1)}), bf16[1024,4096]{1,0:T(8,128)(2,1)}) %all-gather.11.cloned.1.call-update) | async-done | bytes 8388624 | tf_op jit(solution)/shard_map/all_gather | solution.py:235
  406.3 6.7 fusion.155
  413.1 7.0 fusion.125
  466.5 7.2 convolution_convert_fusion.2
  474.9 5.9 convolution_convert_fusion.3
  482.0 5.6 convolution_convert_fusion
  488.9 5.6 convolution_convert_fusion.1
  517.6 61.1 %reduce-scatter.29.cloned.1.call-done = bf16[512,3072]{1,0:T(8,128)(2,1)} async-done(((bf16[1024,3072]{1,0:T(8,128)(2,1)}), bf16[512,3072]{1,0:T(8,128)(2,1)}) %reduce-scatter.29.cloned.1.call-update) | async-done | bytes 3145744 | tf_op jit(solution)/shard_map/reduce_scatter | solution.py:250
  578.6 79.5 %reduce-scatter.27.cloned.1.call-done = bf16[512,3072]{1,0:T(8,128)(2,1)} async-done(((bf16[1024,3072]{1,0:T(8,128)(2,1)}), bf16[512,3072]{1,0:T(8,128)(2,1)}) %reduce-scatter.27.cloned.1.call-update) | async-done | bytes 3145744 | tf_op jit(solution)/shard_map/reduce_scatter | solution.py:250
  658.1 5.7 add_convert_fusion.2
  663.8 96.6 %reduce-scatter.37.cloned.1.call-done = bf16[512,4096]{1,0:T(8,128)(2,1)} async-done(((bf16[1024,4096]{1,0:T(8,128)(2,1)}), bf16[512,4096]{1,0:T(8,128)(2,1)}) %reduce-scatter.37.cloned.1.call-update) | async-done | bytes 4194320 | tf_op jit(solution)/shard_map/reduce_scatter | solution.py:256
  760.4 102.1 %reduce-scatter.35.cloned.1.call-done = bf16[512,4096]{1,0:T(8,128)(2,1)} async-done(((bf16[1024,4096]{1,0:T(8,128)(2,1)}), bf16[512,4096]{1,0:T(8,128)(2,1)}) %reduce-scatter.35.cloned.1.call-update) | async-done | bytes 4194320 | tf_op jit(solution)/shard_map/reduce_scatter | solution.py:256
  862.4 7.2 add_convert_fusion.1
  869.7 94.4 %reduce-scatter.41.cloned.1.call-done = bf16[2048,1024]{1,0:T(8,128)(2,1)} async-done(((bf16[4096,1024]{1,0:T(8,128)(2,1)}), bf16[2048,1024]{1,0:T(8,128)(2,1)}) %reduce-scatter.41.cloned.1.call-update) | async-done | bytes 4194320 | tf_op jit(solution)/shard_map/reduce_scatter | solution.py:259
  964.1 101.5 %reduce-scatter.39.cloned.1.call-done = bf16[2048,1024]{1,0:T(8,128)(2,1)} async-done(((bf16[4096,1024]{1,0:T(8,128)(2,1)}), bf16[2048,1024]{1,0:T(8,128)(2,1)}) %reduce-scatter.39.cloned.1.call-update) | async-done | bytes 4194320 | tf_op jit(solution)/shard_map/reduce_scatter | solution.py:259
  1065.6 7.6 add_convert_fusion
  1075.1 6.9 all-reduce.4
  1085.2 8.4 reduce-scatter.43.cloned.1.call-done
  1094.5 12.9 reduce-scatter.49.cloned.1.call-done
  1108.4 12.9 reduce-scatter.47.cloned.1.call-done
  1122.3 12.9 reduce-scatter.53.cloned.1.call-done
  1136.2 12.9 reduce-scatter.51.cloned.1.call-done
  1150.1 64.1 %all-reduce.2 = (bf16[4,512]{1,0:T(4,128)(2,1)S(1)}, bf16[4,512]{1,0:T(4,128)(2,1)S(1)}, bf16[4,512]{1,0:T(4,128)(2,1)S(1)}, bf16[2048]{0:T(1024)(128)(2,1)S(1)}) all-reduce(bf16[4,512]{1,0:T(4,128)(2,1)S(1)} %add_convert_fusion.19, bf16[4,512]{1,0:T(4,128)(2,1)S(1)} %add_convert_fusion.18, ...), channel_id=1, replica_groups=mesh['wide'=16,'narrow'=2] {'wide'}, use_global_device_ids=true, to_apply=%region_49.50 | all-reduce | flops 8192 | bytes 32768 | tf_op jit(solution)/shard_map/psum | solution.py:274
  1216.6 170.5 %all-reduce.7.cloned.1.call-done = (bf16[512,3072]{1,0:T(8,128)(2,1)}, bf16[512,1024]{1,0:T(8,128)(2,1)}, bf16[512,4096]{1,0:T(8,128)(2,1)}, bf16[2048,1024]{1,0:T(8,128)(2,1)}) async-done(((bf16[512,3072]{1,0:T(8,128)(2,1)}, bf16[512,1024]{1,0:T(8,128)(2,1)}, bf16[512,4096]{1,0:T(8,128)(2,1)}, bf16[2048,1024]{1,0:T(8,128)(2,1)}), (bf16[512,3072]{1,0:T(8,128)(2,1)}, bf16[512,1024]{1,0:T(8,128)(2,1)}, ...) | async-done | bytes 12582928 | tf_op jit(solution)/shard_map/psum | solution.py:276
  1387.1 5.5 convert_element_type.454
  (362 shorter events, 154.7 us)
Async XLA Ops:
  7.2 201.6 %all-gather.5.cloned.1.call-start = ((), (), s32[]{:S(2)}) async-start(), calls=%async_computation.14 | async-start | bytes 9437184 | tf_op jit(solution)/shard_map/all_gather | solution.py:221
  7.9 217.7 %all-gather.7.cloned.1.call-start = ((), (), s32[]{:S(2)}) async-start(), calls=%async_computation.15 | async-start | bytes 3145728 | tf_op jit(solution)/shard_map/all_gather | solution.py:222
  8.7 292.2 %all-gather.9.cloned.1.call-start = ((), (), s32[]{:S(2)}) async-start(), calls=%async_computation.16 | async-start | bytes 12582912 | tf_op jit(solution)/shard_map/all_gather | solution.py:224
  9.4 396.9 %all-gather.11.cloned.1.call-start = ((), (), s32[]{:S(2)}) async-start(), calls=%async_computation.17 | async-start | bytes 12582912 | tf_op jit(solution)/shard_map/all_gather | solution.py:235
  9.5 161.5 %copy-start.54 = (bf16[4,512]{1,0:T(4,128)(2,1)S(1)}, bf16[4,512]{1,0:T(4,128)(2,1)}, u32[]{:S(2)}) copy-start(bf16[4,512]{1,0:T(4,128)(2,1)} %param.22) | copy-start | bytes 12292
  9.5 166.0 %copy-start.55 = (bf16[4,512]{1,0:T(4,128)(2,1)S(1)}, bf16[4,512]{1,0:T(4,128)(2,1)}, u32[]{:S(2)}) copy-start(bf16[4,512]{1,0:T(4,128)(2,1)} %param.17) | copy-start | bytes 12292
  9.5 170.6 %copy-start.56 = (bf16[4,512]{1,0:T(4,128)(2,1)S(1)}, bf16[4,512]{1,0:T(4,128)(2,1)}, u32[]{:S(2)}) copy-start(bf16[4,512]{1,0:T(4,128)(2,1)} %param.16) | copy-start | bytes 12292
  9.5 175.1 %copy-start.65 = (s32[16]{0:T(128)S(1)}, s32[16]{0:T(128)}, u32[]{:S(2)}) copy-start(s32[16]{0:T(128)} %param.15) | copy-start | bytes 196
  9.5 175.1 %copy-start.66 = (s32[2,1]{0,1:T(1,128)S(1)}, s32[2,1]{0,1:T(1,128)}, u32[]{:S(2)}) copy-start(s32[2,1]{0,1:T(1,128)} %param.14) | copy-start | bytes 28
  9.5 176.1 %copy-start.2 = (bf16[2,1,128,1024]{3,2,1,0:T(8,128)(2,1)S(1)}, bf16[2,1,128,1024]{3,2,1,0:T(8,128)(2,1)}, u32[]{:S(2)}) copy-start(bf16[2,1,128,1024]{3,2,1,0:T(8,128)(2,1)} %param.12) | copy-start | bytes 1572868
  9.5 177.1 %collective-permute-start = (bf16[1,512,4096]{2,1,0:T(8,128)(2,1)}, bf16[1,512,4096]{2,1,0:T(8,128)(2,1)}, u32[]{:S(2)}, u32[]{:S(2)}) collective-permute-start(bf16[1,512,4096]{2,1,0:T(8,128)(2,1)} %bitcast.292), channel_id=1, source_target_pairs={{0,1},{1,0},{2,3},{3,2},{4,5},{5,4},{6,7},{7,6},{8,9},{9,8},{10,11... | collective-permute-start | bytes 12582920 | tf_op jit(solution)/shard_map/ppermute | solution.py:23
  12.6 502.1 %reduce-scatter.33.cloned.1.call-start = ((), (), s32[]{:S(2)}) async-start(), calls=%async_computation.21 | async-start | bytes 3145728 | tf_op jit(solution)/shard_map/reduce_scatter | solution.py:253
  213.6 11.4 copy-start.20
  233.3 23.5 %slice-start.2 = ((s8[8388608]{0:T(1024)(128)(4,1)}), s8[4194304]{0:T(1024)(128)(4,1)S(1)}, s32[]{:S(2)}) async-start(s8[8388608]{0:T(1024)(128)(4,1)} %bitcast.295), calls=%async_computation.35 | async-start | bytes 8388608
  233.8 23.0 %copy-start.3 = (f32[128,1024]{1,0:T(8,128)}, f32[128,1024]{1,0:T(8,128)S(1)}, u32[]{:S(2)}) copy-start(f32[128,1024]{1,0:T(8,128)S(1)} %get-tuple-element.93) | copy-start | bytes 1572868
  234.2 22.5 %slice-start.3 = ((s8[8388608]{0:T(1024)(128)(4,1)}), s8[4194304]{0:T(1024)(128)(4,1)S(1)}, s32[]{:S(2)}) async-start(s8[8388608]{0:T(1024)(128)(4,1)} %bitcast.295), calls=%async_computation.36 | async-start | bytes 8388608
  314.9 98.2 %copy-start.42 = (bf16[128,1024]{1,0:T(8,128)(2,1)}, bf16[128,1024]{1,0:T(8,128)(2,1)S(1)}, u32[]{:S(2)}) copy-start(bf16[128,1024]{1,0:T(8,128)(2,1)S(1)} %get-tuple-element.63) | copy-start | bytes 786436
  406.3 14.8 %slice-start = ((s8[8388608]{0:T(1024)(128)(4,1)}), s8[4194304]{0:T(1024)(128)(4,1)S(1)}, s32[]{:S(2)}) async-start(s8[8388608]{0:T(1024)(128)(4,1)} %bitcast.290), calls=%async_computation.33 | async-start | bytes 8388608
  432.5 82.2 %reduce-scatter.31.cloned.1.call-start = ((), (), s32[]{:S(2)}) async-start(), calls=%async_computation.20 | async-start | bytes 3145728 | tf_op jit(solution)/shard_map/reduce_scatter | solution.py:253
  436.8 141.9 %reduce-scatter.29.cloned.1.call-start = ((), (), s32[]{:S(2)}) async-start(), calls=%async_computation.19 | async-start | bytes 9437184 | tf_op jit(solution)/shard_map/reduce_scatter | solution.py:250
  453.0 205.1 %reduce-scatter.27.cloned.1.call-start = ((), (), s32[]{:S(2)}) async-start(), calls=%async_computation.18 | async-start | bytes 9437184 | tf_op jit(solution)/shard_map/reduce_scatter | solution.py:250
  465.5 294.9 %reduce-scatter.37.cloned.1.call-start = ((), (), s32[]{:S(2)}) async-start(), calls=%async_computation.23 | async-start | bytes 12582912 | tf_op jit(solution)/shard_map/reduce_scatter | solution.py:256
  473.7 388.7 %reduce-scatter.35.cloned.1.call-start = ((), (), s32[]{:S(2)}) async-start(), calls=%async_computation.22 | async-start | bytes 12582912 | tf_op jit(solution)/shard_map/reduce_scatter | solution.py:256
  480.8 483.3 %reduce-scatter.41.cloned.1.call-start = ((), (), s32[]{:S(2)}) async-start(), calls=%async_computation.25 | async-start | bytes 12582912 | tf_op jit(solution)/shard_map/reduce_scatter | solution.py:259
  487.7 578.0 %reduce-scatter.39.cloned.1.call-start = ((), (), s32[]{:S(2)}) async-start(), calls=%async_computation.24 | async-start | bytes 12582912 | tf_op jit(solution)/shard_map/reduce_scatter | solution.py:259
  494.5 589.6 %reduce-scatter.45.cloned.1.call-start = ((), (), s32[]{:S(2)}) async-start(), calls=%async_computation.27 | async-start | bytes 393216
  508.9 584.6 %reduce-scatter.43.cloned.1.call-start = ((), (), s32[]{:S(2)}) async-start(), calls=%async_computation.26 | async-start | bytes 393216
  509.9 597.5 %reduce-scatter.49.cloned.1.call-start = ((), (), s32[]{:S(2)}) async-start(), calls=%async_computation.29 | async-start | bytes 393216
  511.0 610.3 %reduce-scatter.47.cloned.1.call-start = ((), (), s32[]{:S(2)}) async-start(), calls=%async_computation.28 | async-start | bytes 393216
  512.2 623.0 %reduce-scatter.53.cloned.1.call-start = ((), (), s32[]{:S(2)}) async-start(), calls=%async_computation.31 | async-start | bytes 393216
  513.3 635.7 %reduce-scatter.51.cloned.1.call-start = ((), (), s32[]{:S(2)}) async-start(), calls=%async_computation.30 | async-start | bytes 393216
  514.3 872.7 %all-reduce.7.cloned.1.call-start = ((), (), s32[]{:S(2)}) async-start(), calls=%async_computation.32 | async-start | bytes 25165824 | tf_op jit(solution)/shard_map/psum | solution.py:276
  (64 other events, 218.3 us)
Sparse Core Ops, SparseCore 0:
  9.5 150.5 all-gather.4
  161.7 33.3 all-gather.6
  196.6 104.2 all-gather.8
  302.3 103.9 all-gather.10
  432.6 31.8 reduce-scatter.32
  466.7 31.8 reduce-scatter.30
  501.5 77.1 reduce-scatter.28
  580.9 77.1 reduce-scatter.26
  661.0 99.3 reduce-scatter.36
  763.1 99.3 reduce-scatter.34
  864.7 99.3 reduce-scatter.40
  966.2 99.3 reduce-scatter.38
  1067.8 11.7 reduce-scatter.44
  1081.7 11.7 reduce-scatter.42
  1095.6 11.7 reduce-scatter.48
  1109.5 11.7 reduce-scatter.46
  1123.4 11.7 reduce-scatter.52
  1137.2 11.7 reduce-scatter.50
  1154.2 232.8 all-reduce.6
